TPU v7x, 512 devices: a whole 4x4x16 slice. The times are simulated.
512 devices in a mesh: seq: 64 (over y, z), exp: 8 (over x, core).
Axes of the slice: x: 4, y: 4, z: 16, core: 2. Of those that a mesh axis runs over, the one named last changes fastest.
Arguments:
- tokens: bfloat16 [4096, 128], P('seq'), may hold values from -36 to 36
- norm_gains: float32 [2, 4096], P(None, 'seq'), may hold values from 0.1 to 1.9
- q_weight: bfloat16 [4096, 4096], P('seq', 'exp'), may hold values from -16 to 16
- kv_weight: bfloat16 [4096, 2, 1024], P('seq', None, 'exp'), may hold values from -1 to 1
- out_weight: bfloat16 [4096, 4096], P('seq', 'exp'), may hold values from -0.3 to 0.3
- kv_cache: bfloat16 [2, 512, 256, 1024], P(None, 'seq', None, 'exp'), may hold values from -8 to 8
- block_count: int32 [32], replicated, may hold values from 1 to 128, 512 in all
- placement: int32 [512], P('seq'), may hold values from 0 to 511, each once
- block_live: int32 [512], P('seq'), may hold values 0 or 1
- router_weight: bfloat16 [4096, 8], P('seq'), may hold values from -0.09375 to 0.09375
- routes: int32 [128, 2], replicated, may hold values from 0 to 7, all different within a row
- expert_in: bfloat16 [8, 2, 4096, 7168], P(None, None, 'seq', 'exp'), may hold values from -0.09375 to 0.09375
- expert_out: bfloat16 [8, 4096, 7168], P(None, 'seq', 'exp'), may hold values from -0.0625 to 0.0625
Outputs:
- layer_out: bfloat16 [4096, 128], P('seq')
Inputs may be any that keep to these rules, and one draw needn't show every extreme that they name: `block_count`: the counts sum to 512; the longest request holds exactly 128 blocks. `placement`: each pool slot holds a different block. `routes`: each row names two different experts.
All inputs are finite; a program needn't handle non-finite values. No bound on the sum of `block_live` on one device may be relied on, other than what follows from the above.
Results may differ from a plain program's by a relative error of at most 0.0065.
Values may be sent and summed in bfloat16 or wider, within the bound.
A program may use at most 128 MiB of HBM per device.

v0:
```python
import math
import jax
import jax.numpy as jnp
from jax import lax
from jax.sharding import PartitionSpec as P

D = 4096
HEAD_DIM = 128
TOPK = 2
NEGATIVE = -1e30
EPSILON = 1e-05


def block_owners(block_count, placement):
    starts = jnp.cumsum(block_count) - block_count
    before = (starts[None, :] <= placement[:, None]).astype(jnp.int32)
    return jnp.sum(before, axis=1) - 1


def softmax_join(first_part, second_part):
    joined_top = jnp.maximum(first_part[0], second_part[0])
    first_factor = jnp.exp(first_part[0] - joined_top)
    second_factor = jnp.exp(second_part[0] - joined_top)
    joined_total = first_part[1] * first_factor + second_part[1] * second_factor
    joined_sum = first_part[2] * first_factor[..., None] + second_part[2] * second_factor[..., None]
    return (joined_top, joined_total, joined_sum)


def per_device(
    tokens,
    norm_gains,
    q_weight,
    kv_weight,
    out_weight,
    kv_cache,
    block_count,
    placement,
    block_live,
    router_weight,
    routes,
    expert_in,
    expert_out,
):
    width_dev, row_total = tokens.shape
    requests = block_count.shape[0]
    steps_all = row_total // requests
    kv_heads_dev = kv_cache.shape[3] // HEAD_DIM
    heads_dev = q_weight.shape[1] // HEAD_DIM
    group_size = heads_dev // kv_heads_dev
    blocks_dev = kv_cache.shape[1]
    page_rows = kv_cache.shape[2]
    experts_all = expert_in.shape[0]
    ff_dev = expert_in.shape[3]
    score_scale = 1.0 / math.sqrt(HEAD_DIM)
    contract_first = (((0,), (0,)), ((), ()))
    token_float = tokens.astype(jnp.float32)
    normed = (token_float * norm_gains[0][:, None]).astype(jnp.bfloat16)
    query_part = lax.dot_general(
        normed, q_weight, contract_first, preferred_element_type=jnp.float32
    )
    fresh_part = lax.dot_general(
        normed, kv_weight.reshape(width_dev, -1), contract_first, preferred_element_type=jnp.float32
    )
    first_local = jnp.sum(token_float * token_float, axis=0)
    query_sum, fresh_sum, first_squares = lax.psum((query_part, fresh_part, first_local), "seq")
    attn_rms = lax.rsqrt(first_squares / D + EPSILON)
    queries = (
        (query_sum * attn_rms[:, None])
        .astype(jnp.bfloat16)
        .reshape(steps_all, requests, kv_heads_dev, group_size, HEAD_DIM)
    )
    fresh_rows = (
        (fresh_sum * attn_rms[:, None])
        .astype(jnp.bfloat16)
        .reshape(steps_all, requests, 2, kv_heads_dev, HEAD_DIM)
    )
    new_keys = fresh_rows[:, :, 0]
    new_values = fresh_rows[:, :, 1]
    cache_keys = kv_cache[0].reshape(blocks_dev, page_rows, kv_heads_dev, HEAD_DIM)
    cache_values = kv_cache[1].reshape(blocks_dev, page_rows, kv_heads_dev, HEAD_DIM)
    block_owner = block_owners(block_count, placement)
    block_alive = (block_live == 1)[:, None, None, None]
    member = (block_owner[:, None] == jnp.arange(requests)[None, :])[:, :, None, None, None]

    def attend(query_steps, first_step):
        step_count = query_steps.shape[0]
        picked = query_steps[:, block_owner]
        scores = (
            jnp.einsum("tpkgd,pjkd->pkgtj", picked, cache_keys, preferred_element_type=jnp.float32)
            * score_scale
        )
        block_top = jnp.max(scores, axis=-1)
        weights = jnp.exp(scores - block_top[..., None]).astype(jnp.bfloat16)
        block_total = jnp.sum(weights, axis=-1, dtype=jnp.float32)
        block_sum = jnp.einsum(
            "pkgtj,pjkd->pkgtd", weights, cache_values, preferred_element_type=jnp.float32
        )
        block_top = jnp.where(block_alive, block_top, NEGATIVE)
        block_total = jnp.where(block_alive, block_total, 0.0)
        block_sum = jnp.where(block_alive[..., None], block_sum, 0.0)
        local_top = jnp.max(jnp.where(member, block_top[:, None], NEGATIVE), axis=0)
        factor = jnp.where(
            member, jnp.exp(jnp.where(member, block_top[:, None] - local_top[None], NEGATIVE)), 0.0
        )
        local_total = jnp.sum(factor * block_total[:, None], axis=0)
        local_sum = jnp.einsum(
            "prkgt,pkgtd->rkgtd", factor, block_sum, precision=lax.Precision.HIGHEST
        )
        whole_top = lax.pmax(local_top, "seq")
        rescale = jnp.exp(local_top - whole_top)
        whole_total, whole_sum = lax.psum(
            (local_total * rescale, local_sum * rescale[..., None]), "seq"
        )
        new_scores = (
            jnp.einsum(
                "trkgd,srkd->rkgts", query_steps, new_keys, preferred_element_type=jnp.float32
            )
            * score_scale
        )
        causal = (first_step + jnp.arange(step_count))[:, None] >= jnp.arange(steps_all)[None, :]
        new_scores = jnp.where(causal, new_scores, NEGATIVE)
        new_top = jnp.max(new_scores, axis=-1)
        new_weights = jnp.where(causal, jnp.exp(new_scores - new_top[..., None]), 0.0).astype(
            jnp.bfloat16
        )
        new_total = jnp.sum(new_weights, axis=-1, dtype=jnp.float32)
        new_sum = jnp.einsum(
            "rkgts,srkd->rkgtd", new_weights, new_values, preferred_element_type=jnp.float32
        )
        joined_top, joined_total, joined_sum = softmax_join(
            (whole_top, whole_total, whole_sum), (new_top, new_total, new_sum)
        )
        attended = (joined_sum / joined_total[..., None]).astype(jnp.bfloat16)
        return jnp.transpose(attended, (3, 0, 1, 2, 4)).reshape(
            step_count * requests, heads_dev * HEAD_DIM
        )

    attention = jnp.concatenate(
        [
            attend(queries[step_index : step_index + 1], step_index)
            for step_index in range(steps_all)
        ],
        axis=0,
    )
    head_part = lax.dot_general(
        out_weight, attention, (((1,), (1,)), ((), ())), preferred_element_type=jnp.float32
    )
    residual = token_float + lax.psum(head_part, "exp")
    second_local = jnp.sum(residual * residual, axis=0)
    hidden_in = (residual * norm_gains[1][:, None]).astype(jnp.bfloat16)
    router_part = lax.dot_general(
        router_weight, hidden_in, contract_first, preferred_element_type=jnp.float32
    )
    expert_ids = jnp.arange(experts_all)
    chosen_part = jnp.sum(
        jnp.where(routes[:, :, None] == expert_ids[None, None, :], router_part.T[:, None, :], 0.0),
        axis=2,
    )
    flat_routes = routes.reshape(-1)
    pair_rows = row_total * TOPK
    second_squares, logit_sums = lax.psum((second_local, chosen_part), "seq")
    moe_rms = lax.rsqrt(second_squares / D + EPSILON)
    share_rows = pair_rows // lax.axis_size("seq")
    chosen = routes
    every_expert = lax.dot_general(
        hidden_in, expert_in, (((0,), (2,)), ((), ())), preferred_element_type=jnp.float32
    )
    one_hot = (chosen[:, :, None] == expert_ids[None, None, :]).astype(jnp.float32)
    result = jnp.einsum("ike,iecf->ikcf", one_hot, every_expert, precision=lax.Precision.HIGHEST)
    inputs = lax.psum_scatter(
        result.reshape(lax.axis_size("seq") * share_rows, 2 * ff_dev),
        "seq",
        scatter_dimension=0,
        tiled=True,
    )
    share_scale = lax.dynamic_slice_in_dim(
        jnp.repeat(moe_rms, TOPK), lax.axis_index("seq") * share_rows, share_rows, 0
    )
    inputs = inputs * share_scale[:, None]
    chosen = flat_routes
    product = lax.dot_general(
        expert_out,
        lax.all_gather(
            (jax.nn.silu(inputs[:, :ff_dev]) * inputs[:, ff_dev:]).astype(jnp.bfloat16),
            "seq",
            axis=0,
            tiled=True,
        ),
        (((2,), (1,)), ((), ())),
        preferred_element_type=jnp.float32,
    )
    picked = chosen[None, :] == expert_ids[:, None]
    expert_rows = jnp.sum(jnp.where(picked[:, None, :], product, 0.0), axis=0)
    logits = logit_sums * moe_rms[:, None]
    sigmoids = jax.nn.sigmoid(logits)
    gate_weights = sigmoids / jnp.sum(sigmoids, axis=1, keepdims=True)
    expert_part = jnp.sum(
        expert_rows.reshape(width_dev, row_total, TOPK) * gate_weights[None], axis=2
    )
    expert_total = lax.psum(expert_part.astype(jnp.bfloat16), "exp").astype(jnp.float32)
    return (residual + expert_total).astype(jnp.bfloat16)


def solution(mesh):
    return jax.shard_map(
        per_device,
        mesh=mesh,
        in_specs=(
            P("seq", None),
            P(None, "seq"),
            P("seq", "exp"),
            P("seq", None, "exp"),
            P("seq", "exp"),
            P(None, "seq", None, "exp"),
            P(),
            P("seq"),
            P("seq"),
            P("seq", None),
            P(),
            P(None, None, "seq", "exp"),
            P(None, "seq", "exp"),
        ),
        out_specs=P("seq", None),
        check_vma=False,
    )
```

profile of v0, /device:TPU:8, one launch (start us, length us, event | category | flops | bytes accessed | tf_op | source)
XLA Modules:
  0.0 1136.2 jit_solution(5942021511305152113)
XLA Ops:
  6.5 0.8 slice_bitcast_fusion.1
  7.4 1.9 fusion.120
  9.3 0.7 fusion.58
  10.1 0.7 copy.206
  11.7 0.8 convert_reduce_fusion.8
  12.5 128.0 %psum.106 = f32[128]{0:T(128)S(1)} all-reduce(f32[128]{0:T(128)S(1)} %fusion.58), channel_id=1, replica_groups=mesh['seq'=64,'exp'=8] {'seq'}, use_global_device_ids=true, to_apply=%region_2.0 | all-reduce | flops 128 | bytes 1024 | tf_op jit(solution)/shard_map/psum | solution.py:65
  141.3 0.8 copy.245
  142.0 1.7 fusion.59
  143.7 136.8 %all-reduce.9.cloned.1.call-done = f32[128,512]{1,0:T(8,128)} async-done(((f32[128,512]{1,0:T(8,128)}), f32[128,512]{1,0:T(8,128)}) %all-reduce.9.cloned.1.call-update) | async-done | bytes 262160 | tf_op jit(solution)/shard_map/psum | solution.py:65
  280.5 1.0 multiply_convert_fusion
  282.8 1.3 fusion.162
  288.7 122.6 %all-reduce.4 = (f32[32,1,4,1]{0,2,3,1:T(4,128)S(1)}, f32[32,1,4,1]{0,2,3,1:T(4,128)S(1)}, f32[32,1,4,1]{0,2,3,1:T(4,128)S(1)}, f32[32,1,4,1]{0,2,3,1:T(4,128)S(1)}) all-reduce(f32[32,1,4,1]{0,2,3,1:T(4,128)S(1)} %bitcast.383, f32[32,1,4,1]{0,2,3,1:T(4,128)S(1)} %bitcast.389, ...), channel_id=1, replica_groups=mesh['seq'=64,'exp'=8] {'seq'}, use_global_device_ids=true, to_apply=%region_35.36 | all-reduce | flops 512 | bytes 4096 | tf_op jit(solution)/shard_map/pmax | solution.py:109
  411.3 1.0 fusion.5
  412.3 1.0 fusion.7
  413.4 1.0 fusion.9
  414.4 1.0 fusion.11
  415.5 136.6 %all-reduce.2 = (f32[32,1,4,1]{0,2,3,1:T(4,128)S(1)}, f32[32,1,4,1]{0,2,3,1:T(4,128)S(1)}, f32[32,1,4,1]{0,2,3,1:T(4,128)S(1)}, f32[32,1,4,1]{0,2,3,1:T(4,128)S(1)}) all-reduce(f32[32,1,4,1]{0,2,3,1:T(4,128)S(1)} %get-tuple-element.62, f32[32,1,4,1]{0,2,3,1:T(4,128)S(1)} %get-tuple-element.60, ...), channel_id=1, replica_groups=mesh['seq'=64,'exp'=8] {'seq'}, use_global_device_ids=true, to_apply=%region_40.41 | all-reduce | flops 512 | bytes 4096 | tf_op jit(solution)/shard_map/psum | solution.py:111
  552.1 139.3 %all-reduce.13.cloned.1.call-done = (f32[128,256]{1,0:T(8,128)}, f32[32,1,4,1,128]{4,0,2,3,1:T(8,128)}, f32[32,1,4,1,128]{4,0,2,3,1:T(8,128)}, f32[32,1,4,1,128]{4,0,2,3,1:T(8,128)}, f32[32,1,4,1,128]{4,0,2,3,1:T(8,128)}) async-done(((f32[128,256]{1,0:T(8,128)}, f32[32,1,4,1,128]{4,0,2,3,1:T(8,128)}, f32[32,1,4,1,128]{4,0,2,3,1:T(8,128)}, f32[32,1,4,1,128]{4,0,2,3,1:T(8,128)}, ...) | async-done | bytes 393232 | tf_op jit(solution)/shard_map/psum | solution.py:65
  691.4 1.0 multiply_convert_fusion.1
  693.4 1.0 fusion.49
  697.3 23.6 %psum.116 = f32[64,128]{1,0:T(8,128)S(1)} all-reduce(f32[64,128]{1,0:T(8,128)S(1)} %convolution_bitcast_fusion.5), channel_id=1, replica_groups=mesh['seq'=64,'exp'=8] {'exp'}, use_global_device_ids=true, to_apply=%region_42.43 | all-reduce | flops 8192 | bytes 65536 | tf_op jit(solution)/shard_map/psum | solution.py:148
  721.0 1.1 fusion.70
  722.1 6.5 fusion
  728.7 0.9 copy.248
  729.6 1.3 copy.269
  731.2 1.3 dynamic-slice
  733.7 120.3 %all-reduce.1 = (f32[128]{0:T(128)S(1)}, f32[128,2]{0,1:T(2,128)S(1)}) all-reduce(f32[128]{0:T(128)S(1)} %get-tuple-element.42, f32[128,2]{0,1:T(2,128)S(1)} %copy.252), channel_id=1, replica_groups=mesh['seq'=64,'exp'=8] {'seq'}, use_global_device_ids=true, to_apply=%region_45.46 | all-reduce | flops 384 | bytes 3072 | tf_op jit(solution)/shard_map/psum | solution.py:161
  854.5 149.4 %all-reduce.11.cloned.1.call-done = f32[256,1792]{1,0:T(8,128)} async-done(((f32[256,1792]{1,0:T(8,128)}), f32[256,1792]{1,0:T(8,128)}) %all-reduce.11.cloned.1.call-update) | async-done | bytes 1835024
  1003.9 0.9 dynamic-slice_multiply_fusion
  1004.8 98.4 %all-gather = bf16[64,4,896]{2,1,0:T(4,128)(2,1)S(1)} all-gather(bf16[1,4,896]{2,1,0:T(4,128)(2,1)S(1)} %fusion.118), channel_id=1, replica_groups=mesh['seq'=64,'exp'=8] {'seq'}, dimensions={0}, use_global_device_ids=true | all-gather | bytes 465920 | tf_op jit(solution)/shard_map/all_gather | solution.py:183
  1103.3 1.7 fusion.3
  1105.4 23.6 %psum.119 = bf16[64,128]{1,0:T(8,128)(2,1)S(1)} all-reduce(bf16[64,128]{1,0:T(8,128)(2,1)S(1)} %copy.254), channel_id=1, replica_groups=mesh['seq'=64,'exp'=8] {'exp'}, use_global_device_ids=true, to_apply=%region_51.52 | all-reduce | flops 8192 | bytes 32768 | tf_op jit(solution)/shard_map/psum | solution.py:200
  (128 shorter events, 13.6 us)
Async XLA Ops:
  6.5 714.4 %copy-start = (bf16[8,2,64,896]{3,2,1,0:T(8,128)(2,1)S(1)}, bf16[8,2,64,896]{3,2,1,0:T(8,128)(2,1)}, u32[]{:S(2)}) copy-start(bf16[8,2,64,896]{3,2,1,0:T(8,128)(2,1)} %param.24) | copy-start | bytes 5505028
  6.5 277.6 %copy-start.1 = (bf16[2,8,256,128]{3,2,1,0:T(8,128)(2,1)S(1)}, bf16[2,8,256,128]{3,2,1,0:T(8,128)(2,1)}, u32[]{:S(2)}) copy-start(bf16[2,8,256,128]{3,2,1,0:T(8,128)(2,1)} %param.18) | copy-start | bytes 3145732
  6.5 274.0 %all-reduce.9.cloned.1.call-start = ((), (), s32[]{:S(2)}) async-start(), calls=%async_computation | async-start | bytes 524288 | tf_op jit(solution)/shard_map/psum | solution.py:65
  9.3 682.1 %all-reduce.13.cloned.1.call-start = ((), (), s32[]{:S(2)}) async-start(), calls=%async_computation.2 | async-start | bytes 786432 | tf_op jit(solution)/shard_map/psum | solution.py:65
  415.4 588.5 %all-reduce.11.cloned.1.call-start = ((), (), s32[]{:S(2)}) async-start(), calls=%async_computation.1 | async-start | bytes 3670016
  691.4 3.7 copy-start.5
  691.4 4.6 copy-start.4
  692.5 4.5 copy-start.3
  692.6 4.5 copy-start.7
  693.1 27.8 %copy-start.2 = (bf16[64,128]{1,0:T(8,128)(2,1)S(1)}, bf16[64,128]{1,0:T(8,128)(2,1)}, u32[]{:S(2)}) copy-start(bf16[64,128]{1,0:T(8,128)(2,1)} %param.13) | copy-start | bytes 49156
  731.0 2.1 copy-start.6
Sparse Core Ops, SparseCore 0:
  10.8 269.7 all-reduce.8
  415.5 275.8 all-reduce.12
  731.1 272.7 all-reduce.10
where the time goes:
time: 1140 us
  blocking collectives  653 us (57%)
  waiting for transfers between devices  426 us (37%)
  matrix products  22.1 us (2%)
  between operations  14.3 us (1%)
    psum x2, waiting for transfers between devices, per_device(): lax.psum((query_part, fresh_part, first_local), 'seq')  276 us
    unnamed x4, waiting for transfers between devices  149 us
    psum x1, blocking collectives, attend(): lax.psum((local_total * rescale, local_sum * rescale[..., None]), 'seq')  137 us
    psum x1, blocking collectives, per_device(): lax.psum((query_part, fresh_part, first_local), 'seq')  128 us
    pmax x1, blocking collectives, attend(): whole_top = lax.pmax(local_top, 'seq')  123 us
    psum x1, blocking collectives, per_device(): second_squares, logit_sums = lax.psum((second_local, chosen_part), 'seq')  120 us
    all_gather x1, blocking collectives, per_device(): lax.all_gather((jax.nn.silu(inputs[:, :ff_dev]) * inputs[:, ff_dev:]).ast...  98.4 us
    psum x1, blocking collectives, per_device(): residual = token_float + lax.psum(head_part, 'exp')  23.6 us
  transfers between devices with their start and end apart: 3, of which 3 were waited for; matrix products, arithmetic and copies ran while one was open for 1% of the time, Pallas kernels for 0%

commit v1 on v0

--- a/solution.py
+++ b/solution.py
@@ -180,11 +180,17 @@
     chosen = flat_routes
     product = lax.dot_general(
         expert_out,
-        lax.all_gather(
-            (jax.nn.silu(inputs[:, :ff_dev]) * inputs[:, ff_dev:]).astype(jnp.bfloat16),
-            "seq",
+        jnp.concatenate(
+            lax.all_to_all(
+                jnp.stack(
+                    [(jax.nn.silu(inputs[:, :ff_dev]) * inputs[:, ff_dev:]).astype(jnp.bfloat16)]
+                    * lax.axis_size("seq")
+                ),
+                "seq",
+                0,
+                0,
+            ),
             axis=0,
-            tiled=True,
         ),
         (((2,), (1,)), ((), ())),
         preferred_element_type=jnp.float32,

time: 1140 us -> 1070 us (0.939)
  blocking collectives: 653 us -> 555 us
  waiting for transfers between devices: 426 us -> 446 us
    all_gather x1 -> x0, blocking collectives: 98.4 us -> none  [per_device(): lax.all_gather((jax.nn.silu(inputs[:, :ff_dev]) * inputs[:, ff_dev:]).ast...]
    all_to_all x0 -> x1, waiting for transfers between devices: none -> 20.4 us  [per_device(): lax.all_to_all(jnp.stack([(jax.nn.silu(inputs[:, :ff_dev]) * inputs[:, ff...]
  transfers between devices with their start and end apart: 3 -> 4, of which waited for: 3 -> 4; matrix products, arithmetic and copies ran while one was open for 1% -> 1% of each run, Pallas kernels for 0% -> 0%
where the time goes in v1:
time: 1070 us
  blocking collectives  555 us (52%)
  waiting for transfers between devices  446 us (42%)
  matrix products  22.1 us (2%)
  between operations  14.3 us (1%)
  local copies, waits for them, and re-layouts  11.8 us (1%)
    psum x2, waiting for transfers between devices, per_device(): lax.psum((query_part, fresh_part, first_local), 'seq')  276 us
    unnamed x4, waiting for transfers between devices  150 us
    psum x1, blocking collectives, attend(): lax.psum((local_total * rescale, local_sum * rescale[..., None]), 'seq')  137 us
    psum x1, blocking collectives, per_device(): lax.psum((query_part, fresh_part, first_local), 'seq')  128 us
    pmax x1, blocking collectives, attend(): whole_top = lax.pmax(local_top, 'seq')  123 us
    psum x1, blocking collectives, per_device(): second_squares, logit_sums = lax.psum((second_local, chosen_part), 'seq')  120 us
    psum x1, blocking collectives, per_device(): residual = token_float + lax.psum(head_part, 'exp')  23.6 us
    psum x1, blocking collectives, per_device(): lax.psum(expert_part.astype(jnp.bfloat16), 'exp').astype(jnp.float32)  23.6 us
  transfers between devices with their start and end apart: 4, of which 4 were waited for; matrix products, arithmetic and copies ran while one was open for 1% of the time, Pallas kernels for 0%

profile of v1, /device:TPU:8, one launch (start us, length us, event | category | flops | bytes accessed | tf_op | source)
XLA Modules:
  0.0 1069.5 jit_solution(13972998597743066660)
XLA Ops:
  6.5 0.8 slice_bitcast_fusion.1
  7.4 1.9 fusion.119
  11.7 0.8 convert_reduce_fusion.8
  12.5 128.0 %psum.106 = f32[128]{0:T(128)S(1)} all-reduce(f32[128]{0:T(128)S(1)} %fusion.58), channel_id=1, replica_groups=mesh['seq'=64,'exp'=8] {'seq'}, use_global_device_ids=true, to_apply=%region_2.0 | all-reduce | flops 128 | bytes 1024 | tf_op jit(solution)/shard_map/psum | solution.py:65
  141.3 0.8 copy.245
  142.0 1.7 fusion.59
  143.7 136.8 %all-reduce.9.cloned.1.call-done = f32[128,512]{1,0:T(8,128)} async-done(((f32[128,512]{1,0:T(8,128)}), f32[128,512]{1,0:T(8,128)}) %all-reduce.9.cloned.1.call-update) | async-done | bytes 262160 | tf_op jit(solution)/shard_map/psum | solution.py:65
  280.5 1.0 multiply_convert_fusion
  282.8 1.3 fusion.161
  288.7 122.6 %all-reduce.4 = (f32[32,1,4,1]{0,2,3,1:T(4,128)S(1)}, f32[32,1,4,1]{0,2,3,1:T(4,128)S(1)}, f32[32,1,4,1]{0,2,3,1:T(4,128)S(1)}, f32[32,1,4,1]{0,2,3,1:T(4,128)S(1)}) all-reduce(f32[32,1,4,1]{0,2,3,1:T(4,128)S(1)} %bitcast.381, f32[32,1,4,1]{0,2,3,1:T(4,128)S(1)} %bitcast.387, ...), channel_id=1, replica_groups=mesh['seq'=64,'exp'=8] {'seq'}, use_global_device_ids=true, to_apply=%region_35.36 | all-reduce | flops 512 | bytes 4096 | tf_op jit(solution)/shard_map/pmax | solution.py:109
  411.3 1.0 fusion.5
  412.3 1.0 fusion.7
  413.4 1.0 fusion.9
  414.4 1.0 fusion.11
  415.5 136.6 %all-reduce.2 = (f32[32,1,4,1]{0,2,3,1:T(4,128)S(1)}, f32[32,1,4,1]{0,2,3,1:T(4,128)S(1)}, f32[32,1,4,1]{0,2,3,1:T(4,128)S(1)}, f32[32,1,4,1]{0,2,3,1:T(4,128)S(1)}) all-reduce(f32[32,1,4,1]{0,2,3,1:T(4,128)S(1)} %get-tuple-element.62, f32[32,1,4,1]{0,2,3,1:T(4,128)S(1)} %get-tuple-element.60, ...), channel_id=1, replica_groups=mesh['seq'=64,'exp'=8] {'seq'}, use_global_device_ids=true, to_apply=%region_40.41 | all-reduce | flops 512 | bytes 4096 | tf_op jit(solution)/shard_map/psum | solution.py:111
  552.1 139.3 %all-reduce.13.cloned.1.call-done = (f32[128,256]{1,0:T(8,128)}, f32[32,1,4,1,128]{4,0,2,3,1:T(8,128)}, f32[32,1,4,1,128]{4,0,2,3,1:T(8,128)}, f32[32,1,4,1,128]{4,0,2,3,1:T(8,128)}, f32[32,1,4,1,128]{4,0,2,3,1:T(8,128)}) async-done(((f32[128,256]{1,0:T(8,128)}, f32[32,1,4,1,128]{4,0,2,3,1:T(8,128)}, f32[32,1,4,1,128]{4,0,2,3,1:T(8,128)}, f32[32,1,4,1,128]{4,0,2,3,1:T(8,128)}, ...) | async-done | bytes 393232 | tf_op jit(solution)/shard_map/psum | solution.py:65
  691.4 1.0 multiply_convert_fusion.1
  693.4 1.0 fusion.49
  697.3 23.6 %psum.116 = f32[64,128]{1,0:T(8,128)S(1)} all-reduce(f32[64,128]{1,0:T(8,128)S(1)} %convolution_bitcast_fusion.5), channel_id=1, replica_groups=mesh['seq'=64,'exp'=8] {'exp'}, use_global_device_ids=true, to_apply=%region_42.43 | all-reduce | flops 8192 | bytes 65536 | tf_op jit(solution)/shard_map/psum | solution.py:148
  721.0 1.1 fusion.70
  722.1 6.5 fusion
  728.7 0.9 copy.248
  729.6 1.3 copy.269
  731.0 1.3 dynamic-slice
  733.5 120.3 %all-reduce.1 = (f32[128]{0:T(128)S(1)}, f32[128,2]{0,1:T(2,128)S(1)}) all-reduce(f32[128]{0:T(128)S(1)} %get-tuple-element.42, f32[128,2]{0,1:T(2,128)S(1)} %copy.252), channel_id=1, replica_groups=mesh['seq'=64,'exp'=8] {'seq'}, use_global_device_ids=true, to_apply=%region_45.46 | all-reduce | flops 384 | bytes 3072 | tf_op jit(solution)/shard_map/psum | solution.py:161
  854.2 149.5 %all-reduce.11.cloned.1.call-done = f32[256,1792]{1,0:T(8,128)} async-done(((f32[256,1792]{1,0:T(8,128)}), f32[256,1792]{1,0:T(8,128)}) %all-reduce.11.cloned.1.call-update) | async-done | bytes 1835024
  1003.7 0.9 dynamic-slice_multiply_fusion
  1004.7 0.9 stack.2
  1005.6 10.3 all-to-all-start
  1016.1 20.4 %all-to-all-done = bf16[64,4,896]{2,1,0:T(4,128)(2,1)S(1)} async-done(((bf16[64,4,896]{2,1,0:T(4,128)(2,1)}), bf16[64,4,896]{2,1,0:T(4,128)(2,1)S(1)}, u32[]{:S(2)}, u32[]{:S(2)}) %all-to-all-start) | async-done | bytes 458784 | tf_op jit(solution)/shard_map/all_to_all | solution.py:184
  1036.6 1.7 fusion.3
  1038.7 23.6 %psum.119 = bf16[64,128]{1,0:T(8,128)(2,1)S(1)} all-reduce(bf16[64,128]{1,0:T(8,128)(2,1)S(1)} %copy.254), channel_id=1, replica_groups=mesh['seq'=64,'exp'=8] {'exp'}, use_global_device_ids=true, to_apply=%region_51.52 | all-reduce | flops 8192 | bytes 32768 | tf_op jit(solution)/shard_map/psum | solution.py:206
  (130 shorter events, 15.1 us)
Async XLA Ops:
  6.5 714.4 %copy-start = (bf16[8,2,64,896]{3,2,1,0:T(8,128)(2,1)S(1)}, bf16[8,2,64,896]{3,2,1,0:T(8,128)(2,1)}, u32[]{:S(2)}) copy-start(bf16[8,2,64,896]{3,2,1,0:T(8,128)(2,1)} %param.24) | copy-start | bytes 5505028
  6.5 277.6 %copy-start.1 = (bf16[2,8,256,128]{3,2,1,0:T(8,128)(2,1)S(1)}, bf16[2,8,256,128]{3,2,1,0:T(8,128)(2,1)}, u32[]{:S(2)}) copy-start(bf16[2,8,256,128]{3,2,1,0:T(8,128)(2,1)} %param.18) | copy-start | bytes 3145732
  6.5 274.0 %all-reduce.9.cloned.1.call-start = ((), (), s32[]{:S(2)}) async-start(), calls=%async_computation.1 | async-start | bytes 524288 | tf_op jit(solution)/shard_map/psum | solution.py:65
  9.3 682.1 %all-reduce.13.cloned.1.call-start = ((), (), s32[]{:S(2)}) async-start(), calls=%async_computation.3 | async-start | bytes 786432 | tf_op jit(solution)/shard_map/psum | solution.py:65
  415.4 588.4 %all-reduce.11.cloned.1.call-start = ((), (), s32[]{:S(2)}) async-start(), calls=%async_computation.2 | async-start | bytes 3670016
  691.4 3.7 copy-start.5
  691.4 4.6 copy-start.4
  692.5 4.5 copy-start.3
  692.6 4.5 copy-start.7
  693.1 27.8 %copy-start.2 = (bf16[64,128]{1,0:T(8,128)(2,1)S(1)}, bf16[64,128]{1,0:T(8,128)(2,1)}, u32[]{:S(2)}) copy-start(bf16[64,128]{1,0:T(8,128)(2,1)} %param.13) | copy-start | bytes 49156
  731.0 2.0 copy-start.6
  1005.6 30.9 %all-to-all-start = ((bf16[64,4,896]{2,1,0:T(4,128)(2,1)}), bf16[64,4,896]{2,1,0:T(4,128)(2,1)S(1)}, u32[]{:S(2)}, u32[]{:S(2)}) async-start(bf16[64,4,896]{2,1,0:T(4,128)(2,1)} %stack.2), calls=%async_computation | async-start | bytes 917504 | tf_op jit(solution)/shard_map/all_to_all | solution.py:184
Sparse Core Ops, SparseCore 0:
  10.8 269.7 all-reduce.8
  415.5 275.8 all-reduce.12
  731.1 272.5 all-reduce.10
